TPU v7x, 256 devices: a whole 4x4x8 slice. The times are simulated.
256 devices in a mesh: sub: 32 (over z, x_hi, core), rng: 8 (over y, x_lo).
Axes of the slice: x: 4 (x_hi: 2, x_lo: 2; x = x_hi * 2 + x_lo), y: 4, z: 8, core: 2. Of those that a mesh axis runs over, the one named last changes fastest.
Arguments:
- raw_echoes: bfloat16 [2, 32768, 4096], P(None, ('sub', 'rng')), may hold values from -6 to 6
- merge_taps: int32 [4, 2, 8, 512], replicated, may hold values from 0 to 255
- merge_weights: float32 [4, 2, 8, 512], replicated, may hold values from -2 to 2
- track_offsets: int32 [4, 32], replicated, may hold values from 0 to 63
Outputs:
- despeckled: float32 [8192, 4096], P('sub', 'rng')
All inputs are finite; a program needn't handle non-finite values.
Results may differ from a plain program's by a relative error of at most 0.0045.
Values may be sent and summed in bfloat16 or wider, within the bound.
A program may use at most 64 MiB of HBM per device.

v0:
```python
import functools
import math

import jax
import jax.numpy as jnp
import numpy as np
from jax import lax
from jax.experimental import pallas as pl
from jax.experimental.pallas import tpu as pltpu
from jax.sharding import PartitionSpec as P

FACTOR = 64
ANG = 256
TAPS = 8
MERGES = 4
SWEEPS = 8
PERIOD = 8192
LANES = 128
CHUNKS = 4
GROUPS = 8
MESH = pl.DeviceIdType.MESH

bf16 = jnp.bfloat16
f32 = jnp.float32


def make_tables():
    tile = np.arange(LANES)
    b = np.arange(LANES)
    second = np.zeros((GROUPS, 2, LANES, 2, LANES))
    for g in range(GROUPS):
        r = (tile // 16 - g) % 8
        d = 16 * r + tile % 16
        angle = 2.0 * np.pi / 128.0 * ((b[:, None] * d[None, :]) % 128)
        cosine, sine = np.cos(angle) / FACTOR, np.sin(angle) / FACTOR
        second[g, 0, :, 0] = cosine
        second[g, 1, :, 0] = sine
        second[g, 0, :, 1] = -sine
        second[g, 1, :, 1] = cosine
    second = second.reshape(GROUPS, 2 * LANES, 2 * LANES)
    c = np.arange(32)
    angle = 2.0 * np.pi / 4096.0 * (c[:, None] * b[None, :])
    twiddle = np.stack([np.cos(angle), np.sin(angle)])
    a = np.arange(ANG) - ANG // 2
    q = np.arange(1024)
    angle = 2.0 * np.pi / 1024.0 * ((a[:, None] * q[None, :]) % 1024)
    beam = np.stack([np.cos(angle), np.sin(angle)]) / 32.0
    beam = beam.reshape(2, ANG, 4, 2, LANES).transpose(3, 0, 1, 2, 4)
    return (
        second.astype(jnp.bfloat16),
        twiddle.astype(np.float32),
        np.ascontiguousarray(beam).astype(jnp.bfloat16),
    )


def transform_eight(z):
    half = math.sqrt(0.5)

    def four(v):
        (ar, ai), (br, bi), (cr, ci), (dr, di) = v
        sr, si, tr, ti = ar + cr, ai + ci, ar - cr, ai - ci
        ur, ui, vr, vi = br + dr, bi + di, br - dr, bi - di
        return [(sr + ur, si + ui), (tr + vi, ti - vr), (sr - ur, si - ui), (tr - vi, ti + vr)]

    even = four(z[0::2])
    odd = four(z[1::2])
    (o0r, o0i), (o1r, o1i), (o2r, o2i), (o3r, o3i) = odd
    turned = [
        (o0r, o0i),
        ((o1r + o1i) * half, (o1i - o1r) * half),
        (o2i, -o2r),
        ((o3i - o3r) * half, (-o3i - o3r) * half),
    ]
    low = [(er + tr, ei + ti) for (er, ei), (tr, ti) in zip(even, turned)]
    high = [(er - tr, ei - ti) for (er, ei), (tr, ti) in zip(even, turned)]
    return low + high


def unit_circle(steps):
    moved = steps + 1024
    quadrant = moved >> 11
    x = ((moved & 2047) - 1024).astype(f32) * (2.0 * math.pi / PERIOD)
    z = x * x
    sine = x * (1.0 + z * (-1.0 / 6.0 + z * (1.0 / 120.0 - z * (1.0 / 5040.0))))
    cosine = 1.0 + z * (-0.5 + z * (1.0 / 24.0 + z * (-1.0 / 720.0 + z * (1.0 / 40320.0))))
    swap = (quadrant & 1) == 1
    out_cos = jnp.where(swap, sine, cosine)
    out_sin = jnp.where(swap, cosine, sine)
    out_cos = jnp.where(((quadrant + 1) & 2) == 2, -out_cos, out_cos)
    out_sin = jnp.where((quadrant & 2) == 2, -out_sin, out_sin)
    return out_cos, out_sin


def order_of_steps():
    return [
        ("beam", 0), ("lead", 0), ("m0", 0), ("beam", 1), ("m1", 0), ("lead", 1), ("m0", 1),
        ("m2", 0), ("beam", 2), ("m1", 1), ("lead", 2), ("m0", 2), ("m2", 1), ("m3", 0), ("beam", 3),
        ("m1", 2), ("lead", 3), ("m0", 3), ("m2", 2), ("m3", 1), ("m1", 3), ("m2", 3), ("m3", 2), ("m3", 3),
    ]


def kernel(
    raw_hbm, second_hbm, beam_hbm, twiddle_ref, taps_ref, weights_ref, offsets_ref, out_ref,
    raw, second, beam, left, rows_buf, wide, sent, got, part_out, part_in, part_own,
    image, image_in, own_part, phase, mats, perm, final, halo_out, halo_in,
    in_sem, own_sem, send_a, recv_a, send_x, recv_x, send_m, recv_m, send_h, recv_h,
):
    sub = lax.axis_index("sub")
    rng = lax.axis_index("rng")
    x_lo = rng % 2
    y = rng // 2

    half_bits = [(sub // 2**l) % 2 for l in range(MERGES)]
    partners = [sub + 2**l - 2 * 2**l * half_bits[l] for l in range(MERGES)]
    x_partner = rng + 1 - 2 * x_lo
    y_partners = [((y + j) % 4) * 2 + x_lo for j in (1, 2, 3)]
    halo_partners = [(rng + 7) % 8, (rng + 1) % 8]

    raw_copies = [
        pltpu.make_async_copy(raw_hbm.at[:, pl.ds(64 * h, 64)], raw.at[:, pl.ds(64 * h, 64)], in_sem.at[h])
        for h in range(2)
    ]
    second_copy = pltpu.make_async_copy(second_hbm, second, in_sem.at[2])
    beam_copy = pltpu.make_async_copy(beam_hbm.at[x_lo], beam, in_sem.at[3])
    for copy in raw_copies:
        copy.start()
    second_copy.start()
    beam_copy.start()

    barrier = pltpu.get_barrier_semaphore()
    ids = [{"rng": t} for t in y_partners + [x_partner] + halo_partners] + [{"sub": t} for t in partners]
    for one in ids:
        pl.semaphore_signal(barrier, inc=1, device_id=one, device_id_type=MESH)

    lane = lax.broadcasted_iota(jnp.int32, (16, LANES), 1)
    group_bits = [((lane // 16) // 2**t) % 2 == 1 for t in range(3)]
    a_copies = {}
    own_copies = {}

    def transform(i, first):
        def rows(block, carry):
            at = pl.ds(pl.multiple_of(block * 16, 16), 16)

            def load(part, a):
                return raw[part, at, a * LANES : (a + 1) * LANES].astype(f32)

            mixed = []
            for m in range(8):
                v = [(load(0, m + 8 * j), load(1, m + 8 * j)) for j in range(4)]
                if i % 2 == 0:
                    sr, si = v[0][0] + v[2][0], v[0][1] + v[2][1]
                    tr, ti = v[1][0] + v[3][0], v[1][1] + v[3][1]
                    zr, zi = (sr + tr, si + ti) if i == 0 else (sr - tr, si - ti)
                else:
                    sr, si = v[0][0] - v[2][0], v[0][1] - v[2][1]
                    tr, ti = v[1][0] - v[3][0], v[1][1] - v[3][1]
                    zr, zi = (sr + ti, si - tr) if i == 1 else (sr - ti, si + tr)
                if i * m:
                    turn = 2.0 * math.pi * i * m / 32.0
                    wc, ws = math.cos(turn), math.sin(turn)
                    zr, zi = zr * wc + zi * ws, zi * wc - zr * ws
                mixed.append((zr, zi))
            for g, (zr, zi) in enumerate(transform_eight(mixed)):
                c = i + 4 * g
                wc = twiddle_ref[0, c : c + 1, :]
                ws = twiddle_ref[1, c : c + 1, :]
                rows_buf[g, at, 0:LANES] = (zr * wc + zi * ws).astype(bf16)
                rows_buf[g, at, LANES : 2 * LANES] = (zi * wc - zr * ws).astype(bf16)
            return carry

        if first:
            raw_copies[0].wait()
            lax.fori_loop(0, 4, rows, 0)
            raw_copies[1].wait()
            lax.fori_loop(4, 8, rows, 0)
            second_copy.wait()
        else:
            lax.fori_loop(0, 8, rows, 0)
        for g in range(GROUPS):
            wide[g] = jnp.dot(rows_buf[g], second[g], preferred_element_type=f32)

        def pick(block, carry):
            at = pl.ds(pl.multiple_of(block * 16, 16), 16)
            for part in range(2):
                tiles = [wide[(8 - r) % 8, at, part * LANES : (part + 1) * LANES] for r in range(8)]
                for t in range(3):
                    tiles = [jnp.where(group_bits[t], tiles[(r - 2**t) % 8], tiles[r]) for r in range(8)]
                for r in range(8):
                    sent[i, r // 2, part, at, (r % 2) * LANES : (r % 2 + 1) * LANES] = tiles[r].astype(bf16)
            return carry

        lax.fori_loop(0, 8, pick, 0)
        if first:
            pl.semaphore_wait(barrier, len(ids))
        for j in (2, 1, 3):
            target = (y + j) % 4
            copy = pltpu.make_async_remote_copy(
                src_ref=sent.at[i, target],
                dst_ref=got.at[i, y],
                send_sem=send_a.at[i, j - 1],
                recv_sem=recv_a.at[i, j - 1],
                device_id={"rng": target * 2 + x_lo},
                device_id_type=MESH,
            )
            copy.start()
            a_copies[i, j] = copy
        own_copies[i] = pltpu.make_async_copy(sent.at[i, y], got.at[i, y], own_sem.at[i])
        own_copies[i].start()

    for i in range(CHUNKS):
        transform(i, i == 0)

    beam_copy.wait()
    for t in range(4):
        cosine, sine = beam[0, :, t], beam[1, :, t]
        left[0:ANG, (2 * t) * LANES : (2 * t + 1) * LANES] = cosine
        left[0:ANG, (2 * t + 1) * LANES : (2 * t + 2) * LANES] = sine
        left[ANG:, (2 * t) * LANES : (2 * t + 1) * LANES] = -sine
        left[ANG:, (2 * t + 1) * LANES : (2 * t + 2) * LANES] = cosine

    angle_rows = lax.broadcasted_iota(jnp.int32, (ANG, ANG), 0)
    sector = sub * 0
    for l in range(MERGES):
        bit = half_bits[l]
        for which in range(2):
            half = bit if which == 0 else 1 - bit
            at = pl.ds(pl.multiple_of(bit * ANG, ANG), ANG)
            taps = taps_ref[l, half, :, at]
            weights = weights_ref[l, half, :, at]
            total = jnp.zeros((ANG, ANG), f32)
            for t in range(TAPS):
                total = total + jnp.where(taps[t : t + 1, :] == angle_rows, weights[t : t + 1, :], 0.0)
            mats[l, which] = total.T.astype(bf16)
            offset = offsets_ref[l, sub] if which == 0 else offsets_ref[l, partners[l]]
            anchor = sector * (2 * ANG) + bit * ANG

            def fill(block, carry, l=l, which=which, offset=offset, anchor=anchor):
                start = pl.multiple_of(block * 32, 32)
                at = pl.ds(start, 32)
                row = lax.broadcasted_iota(jnp.int32, (32, LANES), 0)
                col = lax.broadcasted_iota(jnp.int32, (32, LANES), 1)
                column = 512 * rng + 32 * (col & 15) + 4 * (((col >> 4) - rng) & 7) + 1
                slope = (offset * (anchor + start + row)) & (PERIOD - 1)
                er, ei = unit_circle((slope * column) & (PERIOD - 1))
                tr, ti = unit_circle(slope)
                er, ei = er * 0.7071067811865476, ei * 0.7071067811865476
                for i in range(CHUNKS):
                    phase[l, which, i, 0, at] = er
                    phase[l, which, i, 1, at] = ei
                    if i < CHUNKS - 1:
                        er, ei = er * tr - ei * ti, er * ti + ei * tr
                return carry

            lax.fori_loop(0, ANG // 32, fill, 0)
        sector = sector * 2 + bit

    for i in range(CHUNKS):
        from_lane = lax.broadcasted_iota(jnp.int32, (LANES, 512), 0)
        to_lane = lax.broadcasted_iota(jnp.int32, (LANES, 512), 1)
        place = 32 * (from_lane & 15) + 4 * (((from_lane >> 4) - rng) & 7) + i
        perm[i * LANES : (i + 1) * LANES, :] = jnp.where(place == to_lane, 1.0, 0.0).astype(bf16)

    x_copies = {}
    m_copies = {}

    def contribution(l, which, i, ref):
        both = jnp.concatenate([ref[0], ref[1]], axis=1)
        proj = jnp.dot(mats[l, which], both, preferred_element_type=f32)
        pr, pi = proj[:, :LANES], proj[:, LANES:]
        er, ei = phase[l, which, i, 0], phase[l, which, i, 1]
        return pr * er - pi * ei, pr * ei + pi * er

    def pass_on(l, i):
        copy = pltpu.make_async_remote_copy(
            src_ref=image.at[l, i],
            dst_ref=image_in.at[l, i],
            send_sem=send_m.at[l, i],
            recv_sem=recv_m.at[l, i],
            device_id={"sub": partners[l]},
            device_id_type=MESH,
        )
        copy.start()
        m_copies[l, i] = copy
        re, im = contribution(l, 0, i, image.at[l, i])
        own_part[l, i, 0] = re
        own_part[l, i, 1] = im

    def step(kind, i):
        if kind == "beam":
            for j in (1, 2, 3):
                a_copies[i, j].wait_recv()
            own_copies[i].wait()
            total = jnp.dot(left[...], got[i].reshape(1024, 2 * LANES), preferred_element_type=f32)
            low, high = total[:, :LANES], total[:, LANES:]
            is_low = x_lo == 0
            part_out[i] = jnp.where(is_low, high, low).astype(bf16)
            copy = pltpu.make_async_remote_copy(
                src_ref=part_out.at[i],
                dst_ref=part_in.at[i],
                send_sem=send_x.at[i],
                recv_sem=recv_x.at[i],
                device_id={"rng": x_partner},
                device_id_type=MESH,
            )
            copy.start()
            x_copies[i] = copy
            part_own[i] = jnp.where(is_low, low, high)
        elif kind == "lead":
            x_copies[i].wait_recv()
            total = (part_own[i] + part_in[i].astype(f32)).astype(bf16)
            image[0, i, 0] = total[:ANG]
            image[0, i, 1] = total[ANG:]
            pass_on(0, i)
        else:
            l = int(kind[1])
            m_copies[l, i].wait_recv()
            re, im = contribution(l, 1, i, image_in.at[l, i])
            re = (re + own_part[l, i, 0]).astype(bf16)
            im = (im + own_part[l, i, 1]).astype(bf16)
            if l < MERGES - 1:
                image[l + 1, i, 0] = re
                image[l + 1, i, 1] = im
                pass_on(l + 1, i)
            else:
                final[0, :, i * LANES : (i + 1) * LANES] = re
                final[1, :, i * LANES : (i + 1) * LANES] = im

    for kind, i in order_of_steps():
        step(kind, i)

    re = jnp.dot(final[0], perm[...], preferred_element_type=f32)
    im = jnp.dot(final[1], perm[...], preferred_element_type=f32)
    out_ref[...] = jnp.sqrt(re * re + im * im)
    halo_out[0] = out_ref[:, 0:LANES].astype(bf16)
    halo_out[1] = out_ref[:, 512 - LANES : 512].astype(bf16)
    halo_copies = []
    for side in range(2):
        copy = pltpu.make_async_remote_copy(
            src_ref=halo_out.at[side],
            dst_ref=halo_in.at[side],
            send_sem=send_h.at[side],
            recv_sem=recv_h.at[side],
            device_id={"rng": halo_partners[side]},
            device_id_type=MESH,
        )
        copy.start()
        halo_copies.append(copy)
    for copy in halo_copies:
        copy.wait_recv()

    ring = 512 + LANES
    spot = lax.broadcasted_iota(jnp.int32, (16, ring), 1)
    closed = ((spot == ring - 1) & (rng == 0)) | ((spot == 511) & (rng == 7))
    rate = jnp.where(closed, 0.0, 0.5)
    side_lane = lax.broadcasted_iota(jnp.int32, (16, LANES), 1)

    def spread(block, carry):
        at = pl.ds(pl.multiple_of(block * 16, 16), 16)
        edge = jnp.where(side_lane < LANES // 2, halo_in[0, at].astype(f32), halo_in[1, at].astype(f32))
        u = jnp.concatenate([out_ref[at, :], edge], axis=1)
        for sweep in range(SWEEPS):
            diff = pltpu.roll(u, ring - 1, 1) - u
            flux = diff * rate / (1.0 + 0.25 * (diff * diff))
            u = u + (flux - pltpu.roll(flux, 1, 1))
        out_ref[at, :] = u[:, :512]
        return carry

    lax.fori_loop(0, ANG // 16, spread, 0)

    for copy in list(a_copies.values()) + list(x_copies.values()) + list(m_copies.values()) + halo_copies:
        copy.wait_send()


def per_device(raw_echoes, merge_taps, merge_weights, track_offsets):
    second, twiddle, beam = make_tables()
    vmem = pl.BlockSpec(memory_space=pltpu.VMEM)
    smem = pl.BlockSpec(memory_space=pltpu.SMEM)
    anywhere = pl.BlockSpec(memory_space=pl.ANY)
    dma = pltpu.SemaphoreType.DMA
    return pl.pallas_call(
        kernel,
        out_shape=jax.ShapeDtypeStruct((ANG, 512), f32),
        in_specs=[anywhere, anywhere, anywhere, vmem, vmem, vmem, smem],
        out_specs=vmem,
        scratch_shapes=[
            pltpu.VMEM((2, 128, 4096), bf16),
            pltpu.VMEM((GROUPS, 256, 256), bf16),
            pltpu.VMEM((2, ANG, 4, LANES), bf16),
            pltpu.VMEM((2 * ANG, 1024), bf16),
            pltpu.VMEM((GROUPS, 128, 256), bf16),
            pltpu.VMEM((GROUPS, 128, 256), f32),
            pltpu.VMEM((CHUNKS, 4, 2, 128, 2 * LANES), bf16),
            pltpu.VMEM((CHUNKS, 4, 2, 128, 2 * LANES), bf16),
            pltpu.VMEM((CHUNKS, 2 * ANG, LANES), bf16),
            pltpu.VMEM((CHUNKS, 2 * ANG, LANES), bf16),
            pltpu.VMEM((CHUNKS, 2 * ANG, LANES), f32),
            pltpu.VMEM((MERGES, CHUNKS, 2, ANG, LANES), bf16),
            pltpu.VMEM((MERGES, CHUNKS, 2, ANG, LANES), bf16),
            pltpu.VMEM((MERGES, CHUNKS, 2, ANG, LANES), f32),
            pltpu.VMEM((MERGES, 2, CHUNKS, 2, ANG, LANES), f32),
            pltpu.VMEM((MERGES, 2, ANG, ANG), bf16),
            pltpu.VMEM((512, 512), bf16),
            pltpu.VMEM((2, ANG, 512), bf16),
            pltpu.VMEM((2, ANG, LANES), bf16),
            pltpu.VMEM((2, ANG, LANES), bf16),
            dma((4,)),
            dma((CHUNKS,)),
            dma((CHUNKS, 3)),
            dma((CHUNKS, 3)),
            dma((CHUNKS,)),
            dma((CHUNKS,)),
            dma((MERGES, CHUNKS)),
            dma((MERGES, CHUNKS)),
            dma((2,)),
            dma((2,)),
        ],
        compiler_params=pltpu.CompilerParams(
            collective_id=0, has_side_effects=True, vmem_limit_bytes=56 << 20
        ),
        name="backproject",
    )(
        raw_echoes,
        jnp.asarray(second),
        jnp.asarray(beam),
        jnp.asarray(twiddle),
        merge_taps,
        merge_weights,
        track_offsets,
    )


def solution(mesh):
    in_specs = (P(None, ("sub", "rng"), None), P(), P(), P())
    out_specs = P("sub", "rng")
    return jax.shard_map(
        per_device, mesh=mesh, in_specs=in_specs, out_specs=out_specs, check_vma=False
    )
```

profile of v0, /device:TPU:1, one launch (start us, length us, event | category | flops | bytes accessed | tf_op | source)
XLA Modules:
  0.0 102.8 jit_solution(7704219928228822080)
XLA Ops:
  0.0 101.0 %backproject.1 = f32[256,512]{1,0:T(8,128)} custom-call(bf16[2,128,4096]{2,1,0:T(8,128)(2,1)} %raw_hbm.1, bf16[8,256,256]{2,1,0:T(8,128)(2,1)} %constant.6.clone.second_hbm, bf16[2,2,256,4,128]{4,3,2,1,0:T(4,128)(2,1)} %constant.7.clone.beam_hbm, f32[2,32,128]{2,1,0:T(8,128)} %constant.8.clone.twiddle_ref, s32[4,2,8,512]{3,2,1,0:T(8,128)} %taps_ref.1, ...), custom_call_target="tpu_custom_call" | custom-call | tf_op jit(solution)/shard_map/backproject/pallas_call | solution.py:380
  101.0 1.9 %copy.9 = f32[256,512]{1,0:T(8,128)} copy(f32[256,512]{1,0:T(8,128)} %backproject.1) | data formatting | bytes 1048576
where the time goes:
time: 103 us
  Pallas kernels  101 us (98%)
  local copies, waits for them, and re-layouts  1.87 us (2%)
    pallas_call x1, Pallas kernels, per_device(): pl.pallas_call(kernel, out_shape=jax.ShapeDtypeStruct((ANG, 512), f32), i...  101 us

commit v1 on v0

--- a/solution.py
+++ b/solution.py
@@ -102,7 +102,7 @@
 def kernel(
     raw_hbm, second_hbm, beam_hbm, twiddle_ref, taps_ref, weights_ref, offsets_ref, out_ref,
     raw, second, beam, left, rows_buf, wide, sent, got, part_out, part_in, part_own,
-    image, image_in, own_part, phase, mats, perm, final, halo_out, halo_in,
+    image, image_in, own_part, phase, mats, perm, final, level, smooth, halo_out, halo_in,
     in_sem, own_sem, send_a, recv_a, send_x, recv_x, send_m, recv_m, send_h, recv_h,
 ):
     sub = lax.axis_index("sub")
@@ -255,10 +255,11 @@
         sector = sector * 2 + bit
 
     for i in range(CHUNKS):
-        from_lane = lax.broadcasted_iota(jnp.int32, (LANES, 512), 0)
-        to_lane = lax.broadcasted_iota(jnp.int32, (LANES, 512), 1)
-        place = 32 * (from_lane & 15) + 4 * (((from_lane >> 4) - rng) & 7) + i
-        perm[i * LANES : (i + 1) * LANES, :] = jnp.where(place == to_lane, 1.0, 0.0).astype(bf16)
+        row = lax.broadcasted_iota(jnp.int32, (640, LANES), 0)
+        col = lax.broadcasted_iota(jnp.int32, (640, LANES), 1)
+        wanted = (64 * (row & 7) + (row >> 3) - 8) & 511
+        place = 32 * (col & 15) + 4 * (((col >> 4) - rng) & 7) + i
+        perm[:, i * LANES : (i + 1) * LANES] = jnp.where(place == wanted, 1.0, 0.0).astype(bf16)
 
     x_copies = {}
     m_copies = {}
@@ -328,13 +329,17 @@
     for kind, i in order_of_steps():
         step(kind, i)
 
-    re = jnp.dot(final[0], perm[...], preferred_element_type=f32)
-    im = jnp.dot(final[1], perm[...], preferred_element_type=f32)
-    out_ref[...] = jnp.sqrt(re * re + im * im)
-    halo_out[0] = out_ref[:, 0:LANES].astype(bf16)
-    halo_out[1] = out_ref[:, 512 - LANES : 512].astype(bf16)
+    def magnitude(at):
+        re = lax.dot_general(perm[at], final[0], (((1,), (1,)), ((), ())), preferred_element_type=f32)
+        im = lax.dot_general(perm[at], final[1], (((1,), (1,)), ((), ())), preferred_element_type=f32)
+        return jnp.sqrt(re * re + im * im)
+
     halo_copies = []
     for side in range(2):
+        at = slice(0, 64) if side else slice(576, 640)
+        slab = magnitude(at)
+        level[at] = slab
+        halo_out[side] = slab.astype(bf16)
         copy = pltpu.make_async_remote_copy(
             src_ref=halo_out.at[side],
             dst_ref=halo_in.at[side],
@@ -345,27 +350,37 @@
         )
         copy.start()
         halo_copies.append(copy)
+    level[64:576] = magnitude(slice(64, 576))
     for copy in halo_copies:
         copy.wait_recv()
 
-    ring = 512 + LANES
-    spot = lax.broadcasted_iota(jnp.int32, (16, ring), 1)
-    closed = ((spot == ring - 1) & (rng == 0)) | ((spot == 511) & (rng == 7))
-    rate = jnp.where(closed, 0.0, 0.5)
-    side_lane = lax.broadcasted_iota(jnp.int32, (16, LANES), 1)
-
-    def spread(block, carry):
-        at = pl.ds(pl.multiple_of(block * 16, 16), 16)
-        edge = jnp.where(side_lane < LANES // 2, halo_in[0, at].astype(f32), halo_in[1, at].astype(f32))
-        u = jnp.concatenate([out_ref[at, :], edge], axis=1)
+    place = lax.broadcasted_iota(jnp.int32, (8, 8, LANES), 1)
+
+    def backward(v):
+        return jnp.concatenate([v[7 - j : 8 - j] for j in range(8)], axis=0)
+
+    def spread(h, carry):
+        at = pl.ds(pl.multiple_of(h * LANES, LANES), LANES)
+        u = level[:, at].reshape(80, 8, LANES)
+        above = halo_in[0, :, at].astype(f32).reshape(8, 8, LANES)
+        below = halo_in[1, :, at].astype(f32).reshape(8, 8, LANES)
+        below = jnp.where(rng == 0, backward(u[8:16]), below)
+        above = jnp.where(rng == 7, backward(u[64:72]), above)
+        u = jnp.concatenate(
+            [jnp.where(place == 0, below, u[:8]), u[8:72], jnp.where(place == 7, above, u[72:])], axis=0
+        )
         for sweep in range(SWEEPS):
-            diff = pltpu.roll(u, ring - 1, 1) - u
-            flux = diff * rate / (1.0 + 0.25 * (diff * diff))
-            u = u + (flux - pltpu.roll(flux, 1, 1))
-        out_ref[at, :] = u[:, :512]
+            diff = u[1:] - u[:-1]
+            flux = diff / (2.0 + 0.5 * (diff * diff))
+            u = u[1:-1] + (flux[1:] - flux[:-1])
+        smooth[h] = u.reshape(512, LANES)
         return carry
 
-    lax.fori_loop(0, ANG // 16, spread, 0)
+    lax.fori_loop(0, 2, spread, 0)
+    for h in range(2):
+        for pair in range(4):
+            both = [smooth[h, pl.ds(2 * pair + t, 64, stride=8), :] for t in range(2)]
+            out_ref[h * LANES : (h + 1) * LANES, pair * LANES : (pair + 1) * LANES] = jnp.concatenate(both, axis=0).T
 
     for copy in list(a_copies.values()) + list(x_copies.values()) + list(m_copies.values()) + halo_copies:
         copy.wait_send()
@@ -399,10 +414,12 @@
             pltpu.VMEM((MERGES, CHUNKS, 2, ANG, LANES), f32),
             pltpu.VMEM((MERGES, 2, CHUNKS, 2, ANG, LANES), f32),
             pltpu.VMEM((MERGES, 2, ANG, ANG), bf16),
-            pltpu.VMEM((512, 512), bf16),
+            pltpu.VMEM((640, 512), bf16),
             pltpu.VMEM((2, ANG, 512), bf16),
-            pltpu.VMEM((2, ANG, LANES), bf16),
-            pltpu.VMEM((2, ANG, LANES), bf16),
+            pltpu.VMEM((640, ANG), f32),
+            pltpu.VMEM((2, 512, LANES), f32),
+            pltpu.VMEM((2, 64, ANG), bf16),
+            pltpu.VMEM((2, 64, ANG), bf16),
             dma((4,)),
             dma((CHUNKS,)),
             dma((CHUNKS, 3)),

time: 103 us -> 82.8 us (0.80)
  Pallas kernels: 101 us -> 80.7 us
    pallas_call x1, Pallas kernels: 101 us -> 80.7 us  [per_device(): pl.pallas_call(kernel, out_shape=jax.ShapeDtypeStruct((ANG, 512), f32), i...]
where the time goes in v1:
time: 82.8 us; the launch traced here: 82.6 us
  Pallas kernels  80.7 us (97%)
  local copies, waits for them, and re-layouts  1.87 us (2%)
    pallas_call x1, Pallas kernels, per_device(): pl.pallas_call(kernel, out_shape=jax.ShapeDtypeStruct((ANG, 512), f32), i...  80.7 us
    unnamed x1, local copies, waits for them, and re-layouts  1.87 us

profile of v1, /device:TPU:1, one launch (start us, length us, event | category | flops | bytes accessed | tf_op | source)
XLA Modules:
  0.0 82.6 jit_solution(17676757001758957206)
XLA Ops:
  0.0 80.7 %backproject.1 = f32[256,512]{1,0:T(8,128)} custom-call(bf16[2,128,4096]{2,1,0:T(8,128)(2,1)} %raw_hbm.1, bf16[8,256,256]{2,1,0:T(8,128)(2,1)} %constant.6.clone.second_hbm, bf16[2,2,256,4,128]{4,3,2,1,0:T(4,128)(2,1)} %constant.7.clone.beam_hbm, f32[2,32,128]{2,1,0:T(8,128)} %constant.8.clone.twiddle_ref, s32[4,2,8,512]{3,2,1,0:T(8,128)} %taps_ref.1, ...), custom_call_target="tpu_custom_call" | custom-call | tf_op jit(solution)/shard_map/backproject/pallas_call | solution.py:395
  80.7 1.9 %copy.9 = f32[256,512]{1,0:T(8,128)} copy(f32[256,512]{1,0:T(8,128)} %backproject.1) | data formatting | bytes 1048576

commit v2 on v1

--- a/solution.py
+++ b/solution.py
@@ -16,7 +16,8 @@
 SWEEPS = 8
 PERIOD = 8192
 LANES = 128
-CHUNKS = 4
+CHUNKS = 8
+ORDER = (0, 4, 1, 5, 2, 6, 3, 7)
 GROUPS = 8
 MESH = pl.DeviceIdType.MESH
 
@@ -27,17 +28,17 @@
 def make_tables():
     tile = np.arange(LANES)
     b = np.arange(LANES)
-    second = np.zeros((GROUPS, 2, LANES, 2, LANES))
-    for g in range(GROUPS):
-        r = (tile // 16 - g) % 8
-        d = 16 * r + tile % 16
-        angle = 2.0 * np.pi / 128.0 * ((b[:, None] * d[None, :]) % 128)
-        cosine, sine = np.cos(angle) / FACTOR, np.sin(angle) / FACTOR
-        second[g, 0, :, 0] = cosine
-        second[g, 1, :, 0] = sine
-        second[g, 0, :, 1] = -sine
-        second[g, 1, :, 1] = cosine
-    second = second.reshape(GROUPS, 2 * LANES, 2 * LANES)
+    second = np.zeros((4, 2, LANES, 2, LANES))
+    real = tile // 64 == 0
+    for g in range(4):
+        for half in range(2):
+            r = 4 * half + (tile // 16 - g) % 4
+            d = 16 * r + tile % 16
+            angle = 2.0 * np.pi / 128.0 * ((b[:, None] * d[None, :]) % 128)
+            cosine, sine = np.cos(angle) / FACTOR, np.sin(angle) / FACTOR
+            second[g, 0, :, half] = np.where(real, cosine, -sine)
+            second[g, 1, :, half] = np.where(real, sine, cosine)
+    second = second.reshape(4, 2 * LANES, 2 * LANES)
     c = np.arange(32)
     angle = 2.0 * np.pi / 4096.0 * (c[:, None] * b[None, :])
     twiddle = np.stack([np.cos(angle), np.sin(angle)])
@@ -45,7 +46,7 @@
     q = np.arange(1024)
     angle = 2.0 * np.pi / 1024.0 * ((a[:, None] * q[None, :]) % 1024)
     beam = np.stack([np.cos(angle), np.sin(angle)]) / 32.0
-    beam = beam.reshape(2, ANG, 4, 2, LANES).transpose(3, 0, 1, 2, 4)
+    beam = beam.reshape(2, ANG, 4, 2, LANES).transpose(3, 0, 1, 2, 4).reshape(2, 2 * ANG, 512)
     return (
         second.astype(jnp.bfloat16),
         twiddle.astype(np.float32),
@@ -93,16 +94,21 @@
 
 def order_of_steps():
     return [
-        ("beam", 0), ("lead", 0), ("m0", 0), ("beam", 1), ("m1", 0), ("lead", 1), ("m0", 1),
-        ("m2", 0), ("beam", 2), ("m1", 1), ("lead", 2), ("m0", 2), ("m2", 1), ("m3", 0), ("beam", 3),
-        ("m1", 2), ("lead", 3), ("m0", 3), ("m2", 2), ("m3", 1), ("m1", 3), ("m2", 3), ("m3", 2), ("m3", 3),
+        ("beam", 0), ("tab", 3), ("beam", 4), ("tab", 0), ("beam", 1), ("lead", 0), ("tab", 1),
+        ("tab", 2), ("m0", 0), ("beam", 5), ("lead", 1), ("lead", 4), ("m0", 1), ("m0", 4),
+        ("m1", 0), ("beam", 2), ("lead", 5), ("beam", 6), ("m1", 1), ("m2", 0), ("m0", 5),
+        ("m1", 4), ("lead", 2), ("m2", 1), ("m0", 2), ("lead", 6), ("beam", 7), ("m1", 5),
+        ("m0", 6), ("m2", 4), ("beam", 3), ("m1", 2), ("lead", 7), ("m2", 5), ("m0", 7),
+        ("m1", 6), ("lead", 3), ("m2", 2), ("m3", 0), ("m0", 3), ("m1", 7), ("m2", 6),
+        ("m1", 3), ("m2", 7), ("perm", 0), ("m2", 3), ("m3", 5), ("m3", 6), ("m3", 2),
+        ("m3", 7), ("m3", 1), ("m3", 4), ("m3", 3),
     ]
 
 
 def kernel(
     raw_hbm, second_hbm, beam_hbm, twiddle_ref, taps_ref, weights_ref, offsets_ref, out_ref,
-    raw, second, beam, left, rows_buf, wide, sent, got, part_out, part_in, part_own,
-    image, image_in, own_part, phase, mats, perm, final, level, smooth, halo_out, halo_in,
+    raw, second, beam, rows_buf, wide, sent, got, part_out, part_in, part_own,
+    image, image_in, phase, mats, perm, final, level, smooth, halo_out, halo_in,
     in_sem, own_sem, send_a, recv_a, send_x, recv_x, send_m, recv_m, send_h, recv_h,
 ):
     sub = lax.axis_index("sub")
@@ -133,7 +139,7 @@
         pl.semaphore_signal(barrier, inc=1, device_id=one, device_id_type=MESH)
 
     lane = lax.broadcasted_iota(jnp.int32, (16, LANES), 1)
-    group_bits = [((lane // 16) // 2**t) % 2 == 1 for t in range(3)]
+    group_bits = [((lane // 16) // 2**t) % 2 == 1 for t in range(2)]
     a_copies = {}
     own_copies = {}
 
@@ -176,17 +182,20 @@
             second_copy.wait()
         else:
             lax.fori_loop(0, 8, rows, 0)
-        for g in range(GROUPS):
-            wide[g] = jnp.dot(rows_buf[g], second[g], preferred_element_type=f32)
-
+        for odd in range(2):
+            for g in range(4):
+                wide[g] = jnp.dot(rows_buf[2 * g + odd], second[g], preferred_element_type=f32)
+            share(i + 4 * odd, first and odd == 0)
+
+    def share(i, first):
         def pick(block, carry):
             at = pl.ds(pl.multiple_of(block * 16, 16), 16)
             for part in range(2):
-                tiles = [wide[(8 - r) % 8, at, part * LANES : (part + 1) * LANES] for r in range(8)]
-                for t in range(3):
-                    tiles = [jnp.where(group_bits[t], tiles[(r - 2**t) % 8], tiles[r]) for r in range(8)]
-                for r in range(8):
-                    sent[i, r // 2, part, at, (r % 2) * LANES : (r % 2 + 1) * LANES] = tiles[r].astype(bf16)
+                tiles = [wide[(4 - r) % 4, at, part * LANES : (part + 1) * LANES] for r in range(4)]
+                for t in range(2):
+                    tiles = [jnp.where(group_bits[t], tiles[(r - 2**t) % 4], tiles[r]) for r in range(4)]
+                for r in range(4):
+                    sent[i, 2 * part + r // 2, at, (r % 2) * LANES : (r % 2 + 1) * LANES] = tiles[r].astype(bf16)
             return carry
 
         lax.fori_loop(0, 8, pick, 0)
@@ -207,20 +216,15 @@
         own_copies[i] = pltpu.make_async_copy(sent.at[i, y], got.at[i, y], own_sem.at[i])
         own_copies[i].start()
 
-    for i in range(CHUNKS):
+    for i in range(4):
         transform(i, i == 0)
 
-    beam_copy.wait()
-    for t in range(4):
-        cosine, sine = beam[0, :, t], beam[1, :, t]
-        left[0:ANG, (2 * t) * LANES : (2 * t + 1) * LANES] = cosine
-        left[0:ANG, (2 * t + 1) * LANES : (2 * t + 2) * LANES] = sine
-        left[ANG:, (2 * t) * LANES : (2 * t + 1) * LANES] = -sine
-        left[ANG:, (2 * t + 1) * LANES : (2 * t + 2) * LANES] = cosine
-
     angle_rows = lax.broadcasted_iota(jnp.int32, (ANG, ANG), 0)
-    sector = sub * 0
-    for l in range(MERGES):
+    sectors = [sub * 0]
+    for l in range(MERGES - 1):
+        sectors.append(sectors[l] * 2 + half_bits[l])
+
+    def tables(l):
         bit = half_bits[l]
         for which in range(2):
             half = bit if which == 0 else 1 - bit
@@ -232,18 +236,20 @@
                 total = total + jnp.where(taps[t : t + 1, :] == angle_rows, weights[t : t + 1, :], 0.0)
             mats[l, which] = total.T.astype(bf16)
             offset = offsets_ref[l, sub] if which == 0 else offsets_ref[l, partners[l]]
-            anchor = sector * (2 * ANG) + bit * ANG
-
-            def fill(block, carry, l=l, which=which, offset=offset, anchor=anchor):
+            anchor = sectors[l] * (2 * ANG) + bit * ANG
+
+            def fill(block, carry, which=which, offset=offset, anchor=anchor):
                 start = pl.multiple_of(block * 32, 32)
                 at = pl.ds(start, 32)
                 row = lax.broadcasted_iota(jnp.int32, (32, LANES), 0)
                 col = lax.broadcasted_iota(jnp.int32, (32, LANES), 1)
-                column = 512 * rng + 32 * (col & 15) + 4 * (((col >> 4) - rng) & 7) + 1
+                column = 512 * rng + 32 * (col & 15) + 8 * (((col >> 4) - rng) & 3) + 1
                 slope = (offset * (anchor + start + row)) & (PERIOD - 1)
                 er, ei = unit_circle((slope * column) & (PERIOD - 1))
                 tr, ti = unit_circle(slope)
                 er, ei = er * 0.7071067811865476, ei * 0.7071067811865476
+                ei = jnp.where(col < 64, -ei, ei)
+                ti = jnp.where(col < 64, -ti, ti)
                 for i in range(CHUNKS):
                     phase[l, which, i, 0, at] = er
                     phase[l, which, i, 1, at] = ei
@@ -252,24 +258,23 @@
                 return carry
 
             lax.fori_loop(0, ANG // 32, fill, 0)
-        sector = sector * 2 + bit
-
-    for i in range(CHUNKS):
-        row = lax.broadcasted_iota(jnp.int32, (640, LANES), 0)
-        col = lax.broadcasted_iota(jnp.int32, (640, LANES), 1)
-        wanted = (64 * (row & 7) + (row >> 3) - 8) & 511
-        place = 32 * (col & 15) + 4 * (((col >> 4) - rng) & 7) + i
-        perm[:, i * LANES : (i + 1) * LANES] = jnp.where(place == wanted, 1.0, 0.0).astype(bf16)
+
+    def orders():
+        for i in range(CHUNKS):
+            row = lax.broadcasted_iota(jnp.int32, (640, LANES), 0)
+            col = lax.broadcasted_iota(jnp.int32, (640, LANES), 1)
+            wanted = (64 * (row & 7) + (row >> 3) - 8) & 511
+            place = 32 * (col & 15) + 8 * (((col >> 4) - rng) & 3) + i
+            for part in range(2):
+                here = (place == wanted) & ((col >> 6) == part)
+                perm[part, :, i * LANES : (i + 1) * LANES] = jnp.where(here, 1.0, 0.0).astype(bf16)
 
     x_copies = {}
     m_copies = {}
 
     def contribution(l, which, i, ref):
-        both = jnp.concatenate([ref[0], ref[1]], axis=1)
-        proj = jnp.dot(mats[l, which], both, preferred_element_type=f32)
-        pr, pi = proj[:, :LANES], proj[:, LANES:]
-        er, ei = phase[l, which, i, 0], phase[l, which, i, 1]
-        return pr * er - pi * ei, pr * ei + pi * er
+        proj = jnp.dot(mats[l, which], ref[...], preferred_element_type=f32)
+        return proj * phase[l, which, i, 0] + pltpu.roll(proj, 64, 1) * phase[l, which, i, 1]
 
     def pass_on(l, i):
         copy = pltpu.make_async_remote_copy(
@@ -282,17 +287,23 @@
         )
         copy.start()
         m_copies[l, i] = copy
-        re, im = contribution(l, 0, i, image.at[l, i])
-        own_part[l, i, 0] = re
-        own_part[l, i, 1] = im
 
     def step(kind, i):
-        if kind == "beam":
+        if kind == "tab":
+            tables(i)
+        elif kind == "perm":
+            orders()
+        elif kind == "beam":
+            if i == ORDER[0]:
+                beam_copy.wait()
             for j in (1, 2, 3):
                 a_copies[i, j].wait_recv()
             own_copies[i].wait()
-            total = jnp.dot(left[...], got[i].reshape(1024, 2 * LANES), preferred_element_type=f32)
-            low, high = total[:, :LANES], total[:, LANES:]
+            total = jnp.dot(beam[...], got[i].reshape(512, 2 * LANES), preferred_element_type=f32)
+            low, high = [
+                total[:ANG, at] + turned * pltpu.roll(total[ANG:, at], 64, 1)
+                for at in (slice(0, LANES), slice(LANES, 2 * LANES))
+            ]
             is_low = x_lo == 0
             part_out[i] = jnp.where(is_low, high, low).astype(bf16)
             copy = pltpu.make_async_remote_copy(
@@ -308,30 +319,25 @@
             part_own[i] = jnp.where(is_low, low, high)
         elif kind == "lead":
             x_copies[i].wait_recv()
-            total = (part_own[i] + part_in[i].astype(f32)).astype(bf16)
-            image[0, i, 0] = total[:ANG]
-            image[0, i, 1] = total[ANG:]
+            image[0, i] = (part_own[i] + part_in[i].astype(f32)).astype(bf16)
             pass_on(0, i)
         else:
             l = int(kind[1])
             m_copies[l, i].wait_recv()
-            re, im = contribution(l, 1, i, image_in.at[l, i])
-            re = (re + own_part[l, i, 0]).astype(bf16)
-            im = (im + own_part[l, i, 1]).astype(bf16)
+            merged = (contribution(l, 0, i, image.at[l, i]) + contribution(l, 1, i, image_in.at[l, i])).astype(bf16)
             if l < MERGES - 1:
-                image[l + 1, i, 0] = re
-                image[l + 1, i, 1] = im
+                image[l + 1, i] = merged
                 pass_on(l + 1, i)
             else:
-                final[0, :, i * LANES : (i + 1) * LANES] = re
-                final[1, :, i * LANES : (i + 1) * LANES] = im
-
+                final[:, i * LANES : (i + 1) * LANES] = merged
+
+    turned = jnp.where(lax.broadcasted_iota(jnp.int32, (ANG, LANES), 1) < 64, 1.0, -1.0)
     for kind, i in order_of_steps():
         step(kind, i)
 
     def magnitude(at):
-        re = lax.dot_general(perm[at], final[0], (((1,), (1,)), ((), ())), preferred_element_type=f32)
-        im = lax.dot_general(perm[at], final[1], (((1,), (1,)), ((), ())), preferred_element_type=f32)
+        re = lax.dot_general(perm[0, at], final[...], (((1,), (1,)), ((), ())), preferred_element_type=f32)
+        im = lax.dot_general(perm[1, at], final[...], (((1,), (1,)), ((), ())), preferred_element_type=f32)
         return jnp.sqrt(re * re + im * im)
 
     halo_copies = []
@@ -399,23 +405,21 @@
         out_specs=vmem,
         scratch_shapes=[
             pltpu.VMEM((2, 128, 4096), bf16),
-            pltpu.VMEM((GROUPS, 256, 256), bf16),
-            pltpu.VMEM((2, ANG, 4, LANES), bf16),
-            pltpu.VMEM((2 * ANG, 1024), bf16),
+            pltpu.VMEM((4, 256, 256), bf16),
+            pltpu.VMEM((2 * ANG, 512), bf16),
             pltpu.VMEM((GROUPS, 128, 256), bf16),
-            pltpu.VMEM((GROUPS, 128, 256), f32),
-            pltpu.VMEM((CHUNKS, 4, 2, 128, 2 * LANES), bf16),
-            pltpu.VMEM((CHUNKS, 4, 2, 128, 2 * LANES), bf16),
-            pltpu.VMEM((CHUNKS, 2 * ANG, LANES), bf16),
-            pltpu.VMEM((CHUNKS, 2 * ANG, LANES), bf16),
-            pltpu.VMEM((CHUNKS, 2 * ANG, LANES), f32),
-            pltpu.VMEM((MERGES, CHUNKS, 2, ANG, LANES), bf16),
-            pltpu.VMEM((MERGES, CHUNKS, 2, ANG, LANES), bf16),
-            pltpu.VMEM((MERGES, CHUNKS, 2, ANG, LANES), f32),
+            pltpu.VMEM((4, 128, 256), f32),
+            pltpu.VMEM((CHUNKS, 4, 128, 2 * LANES), bf16),
+            pltpu.VMEM((CHUNKS, 4, 128, 2 * LANES), bf16),
+            pltpu.VMEM((CHUNKS, ANG, LANES), bf16),
+            pltpu.VMEM((CHUNKS, ANG, LANES), bf16),
+            pltpu.VMEM((CHUNKS, ANG, LANES), f32),
+            pltpu.VMEM((MERGES, CHUNKS, ANG, LANES), bf16),
+            pltpu.VMEM((MERGES, CHUNKS, ANG, LANES), bf16),
             pltpu.VMEM((MERGES, 2, CHUNKS, 2, ANG, LANES), f32),
             pltpu.VMEM((MERGES, 2, ANG, ANG), bf16),
-            pltpu.VMEM((640, 512), bf16),
-            pltpu.VMEM((2, ANG, 512), bf16),
+            pltpu.VMEM((2, 640, CHUNKS * LANES), bf16),
+            pltpu.VMEM((ANG, CHUNKS * LANES), bf16),
             pltpu.VMEM((640, ANG), f32),
             pltpu.VMEM((2, 512, LANES), f32),
             pltpu.VMEM((2, 64, ANG), bf16),

time: 82.8 us -> 69 us (0.83)
  Pallas kernels: 80.7 us -> 66.3 us
    pallas_call x1, Pallas kernels: 80.7 us -> 66.3 us  [per_device(): pl.pallas_call(kernel, out_shape=jax.ShapeDtypeStruct((ANG, 512), f32), i...]
where the time goes in v2:
time: 69 us; the launch traced here: 68.2 us
  Pallas kernels  66.3 us (96%)
  local copies, waits for them, and re-layouts  1.87 us (3%)
    pallas_call x1, Pallas kernels, per_device(): pl.pallas_call(kernel, out_shape=jax.ShapeDtypeStruct((ANG, 512), f32), i...  66.3 us
    unnamed x1, local copies, waits for them, and re-layouts  1.87 us

profile of v2, /device:TPU:1, one launch (start us, length us, event | category | flops | bytes accessed | tf_op | source)
XLA Modules:
  0.0 68.2 jit_solution(16577277326695694086)
XLA Ops:
  0.0 66.3 %backproject.1 = f32[256,512]{1,0:T(8,128)} custom-call(bf16[2,128,4096]{2,1,0:T(8,128)(2,1)} %raw_hbm.1, bf16[4,256,256]{2,1,0:T(8,128)(2,1)} %constant.6.clone.second_hbm, bf16[2,512,512]{2,1,0:T(8,128)(2,1)} %constant.7.clone.beam_hbm, f32[2,32,128]{2,1,0:T(8,128)} %constant.8.clone.twiddle_ref, s32[4,2,8,512]{3,2,1,0:T(8,128)} %taps_ref.1, ...), custom_call_target="tpu_custom_call" | custom-call | tf_op jit(solution)/shard_map/backproject/pallas_call | solution.py:401
  66.3 1.9 %copy.9 = f32[256,512]{1,0:T(8,128)} copy(f32[256,512]{1,0:T(8,128)} %backproject.1) | data formatting | bytes 1048576

commit v3 on v2

--- a/solution.py
+++ b/solution.py
@@ -17,7 +17,7 @@
 PERIOD = 8192
 LANES = 128
 CHUNKS = 8
-ORDER = (0, 4, 1, 5, 2, 6, 3, 7)
+UNITS = ((0,), (1,), (2,), (3,), (4,), (5,), (6,), (7,))
 GROUPS = 8
 MESH = pl.DeviceIdType.MESH
 
@@ -94,21 +94,22 @@
 
 def order_of_steps():
     return [
-        ("beam", 0), ("tab", 3), ("beam", 4), ("tab", 0), ("beam", 1), ("lead", 0), ("tab", 1),
-        ("tab", 2), ("m0", 0), ("beam", 5), ("lead", 1), ("lead", 4), ("m0", 1), ("m0", 4),
-        ("m1", 0), ("beam", 2), ("lead", 5), ("beam", 6), ("m1", 1), ("m2", 0), ("m0", 5),
-        ("m1", 4), ("lead", 2), ("m2", 1), ("m0", 2), ("lead", 6), ("beam", 7), ("m1", 5),
-        ("m0", 6), ("m2", 4), ("beam", 3), ("m1", 2), ("lead", 7), ("m2", 5), ("m0", 7),
-        ("m1", 6), ("lead", 3), ("m2", 2), ("m3", 0), ("m0", 3), ("m1", 7), ("m2", 6),
-        ("m1", 3), ("m2", 7), ("perm", 0), ("m2", 3), ("m3", 5), ("m3", 6), ("m3", 2),
-        ("m3", 7), ("m3", 1), ("m3", 4), ("m3", 3),
+        ("dft", 0), ("dft", 1), ("dft", 2), ("beam", 0), ("dft", 3), ("tab", 0), ("beam", 1),
+        ("lead", 0), ("tab", 2), ("beam", 2), ("m0", 0), ("tab", 1), ("lead", 1), ("beam", 3),
+        ("m0", 1), ("lead", 2), ("beam", 4), ("m1", 0), ("lead", 3), ("m0", 2), ("beam", 5),
+        ("m1", 1), ("m0", 3), ("m2", 0), ("lead", 4), ("beam", 6), ("m1", 2), ("m0", 4),
+        ("m2", 1), ("lead", 5), ("beam", 7), ("m1", 3), ("m0", 5), ("m2", 2), ("lead", 6),
+        ("tab", 3), ("m1", 4), ("m0", 6), ("m2", 3), ("lead", 7), ("m1", 5), ("m0", 7),
+        ("m2", 4), ("m1", 6), ("m3", 1), ("m2", 5), ("perm", 0), ("m1", 7), ("m3", 0),
+        ("m2", 6), ("m2", 7), ("m3", 5), ("m3", 2), ("m3", 3), ("m3", 6), ("m3", 4),
+        ("m3", 7),
     ]
 
 
 def kernel(
-    raw_hbm, second_hbm, beam_hbm, twiddle_ref, taps_ref, weights_ref, offsets_ref, out_ref,
-    raw, second, beam, rows_buf, wide, sent, got, part_out, part_in, part_own,
-    image, image_in, phase, mats, perm, final, level, smooth, halo_out, halo_in,
+    raw_hbm, second_hbm, beam_hbm, twiddle_hbm, taps_hbm, weights_hbm, offsets_ref, out_ref,
+    raw, second, beam, twiddle_ref, taps_ref, weights_ref, rows_buf, wide, sent, got, part_out, part_in, part_own,
+    image, image_in, phase, mats, perm, final, level, halo_out, halo_in,
     in_sem, own_sem, send_a, recv_a, send_x, recv_x, send_m, recv_m, send_h, recv_h,
 ):
     sub = lax.axis_index("sub")
@@ -128,10 +129,16 @@
     ]
     second_copy = pltpu.make_async_copy(second_hbm, second, in_sem.at[2])
     beam_copy = pltpu.make_async_copy(beam_hbm.at[x_lo], beam, in_sem.at[3])
+    twiddle_copy = pltpu.make_async_copy(twiddle_hbm, twiddle_ref, in_sem.at[4])
+    taps_copy = pltpu.make_async_copy(taps_hbm, taps_ref, in_sem.at[5])
+    weights_copy = pltpu.make_async_copy(weights_hbm, weights_ref, in_sem.at[6])
+    twiddle_copy.start()
     for copy in raw_copies:
         copy.start()
     second_copy.start()
     beam_copy.start()
+    taps_copy.start()
+    weights_copy.start()
 
     barrier = pltpu.get_barrier_semaphore()
     ids = [{"rng": t} for t in y_partners + [x_partner] + halo_partners] + [{"sub": t} for t in partners]
@@ -175,6 +182,7 @@
             return carry
 
         if first:
+            twiddle_copy.wait()
             raw_copies[0].wait()
             lax.fori_loop(0, 4, rows, 0)
             raw_copies[1].wait()
@@ -185,7 +193,7 @@
         for odd in range(2):
             for g in range(4):
                 wide[g] = jnp.dot(rows_buf[2 * g + odd], second[g], preferred_element_type=f32)
-            share(i + 4 * odd, first and odd == 0)
+            share(2 * i + odd, first and odd == 0)
 
     def share(i, first):
         def pick(block, carry):
@@ -195,29 +203,31 @@
                 for t in range(2):
                     tiles = [jnp.where(group_bits[t], tiles[(r - 2**t) % 4], tiles[r]) for r in range(4)]
                 for r in range(4):
-                    sent[i, 2 * part + r // 2, at, (r % 2) * LANES : (r % 2 + 1) * LANES] = tiles[r].astype(bf16)
+                    sent[2 * part + r // 2, i, at, (r % 2) * LANES : (r % 2 + 1) * LANES] = tiles[r].astype(bf16)
             return carry
 
         lax.fori_loop(0, 8, pick, 0)
         if first:
             pl.semaphore_wait(barrier, len(ids))
+        for n, unit in enumerate(UNITS):
+            if unit[-1] == i:
+                send_unit(n, pl.ds(unit[0], len(unit)))
+
+    def send_unit(n, at):
         for j in (2, 1, 3):
             target = (y + j) % 4
             copy = pltpu.make_async_remote_copy(
-                src_ref=sent.at[i, target],
-                dst_ref=got.at[i, y],
-                send_sem=send_a.at[i, j - 1],
-                recv_sem=recv_a.at[i, j - 1],
+                src_ref=sent.at[target, at],
+                dst_ref=got.at[at, y],
+                send_sem=send_a.at[n, j - 1],
+                recv_sem=recv_a.at[n, j - 1],
                 device_id={"rng": target * 2 + x_lo},
                 device_id_type=MESH,
             )
             copy.start()
-            a_copies[i, j] = copy
-        own_copies[i] = pltpu.make_async_copy(sent.at[i, y], got.at[i, y], own_sem.at[i])
-        own_copies[i].start()
-
-    for i in range(4):
-        transform(i, i == 0)
+            a_copies[n, j] = copy
+        own_copies[n] = pltpu.make_async_copy(sent.at[y, at], got.at[at, y], own_sem.at[n])
+        own_copies[n].start()
 
     angle_rows = lax.broadcasted_iota(jnp.int32, (ANG, ANG), 0)
     sectors = [sub * 0]
@@ -225,6 +235,9 @@
         sectors.append(sectors[l] * 2 + half_bits[l])
 
     def tables(l):
+        if l == 0:
+            taps_copy.wait()
+            weights_copy.wait()
         bit = half_bits[l]
         for which in range(2):
             half = bit if which == 0 else 1 - bit
@@ -251,8 +264,8 @@
                 ei = jnp.where(col < 64, -ei, ei)
                 ti = jnp.where(col < 64, -ti, ti)
                 for i in range(CHUNKS):
-                    phase[l, which, i, 0, at] = er
-                    phase[l, which, i, 1, at] = ei
+                    phase[l, which, 2 * (i % 4) + i // 4, 0, at] = er
+                    phase[l, which, 2 * (i % 4) + i // 4, 1, at] = ei
                     if i < CHUNKS - 1:
                         er, ei = er * tr - ei * ti, er * ti + ei * tr
                 return carry
@@ -260,84 +273,118 @@
             lax.fori_loop(0, ANG // 32, fill, 0)
 
     def orders():
-        for i in range(CHUNKS):
+        for i in range(4):
             row = lax.broadcasted_iota(jnp.int32, (640, LANES), 0)
             col = lax.broadcasted_iota(jnp.int32, (640, LANES), 1)
             wanted = (64 * (row & 7) + (row >> 3) - 8) & 511
             place = 32 * (col & 15) + 8 * (((col >> 4) - rng) & 3) + i
+            late = 4 * (col >> 6)
             for part in range(2):
-                here = (place == wanted) & ((col >> 6) == part)
+                here = place + (late if part == 0 else 4 - late) == wanted
                 perm[part, :, i * LANES : (i + 1) * LANES] = jnp.where(here, 1.0, 0.0).astype(bf16)
 
     x_copies = {}
     m_copies = {}
 
-    def contribution(l, which, i, ref):
-        proj = jnp.dot(mats[l, which], ref[...], preferred_element_type=f32)
-        return proj * phase[l, which, i, 0] + pltpu.roll(proj, 64, 1) * phase[l, which, i, 1]
-
-    def pass_on(l, i):
+    def contribution(l, which, unit, ref):
+        proj = jnp.dot(
+            mats[l, which],
+            jnp.concatenate([ref[l, q] for q in unit], axis=1),
+            preferred_element_type=f32,
+        )
+        parts = [proj[:, t * LANES : (t + 1) * LANES] for t in range(len(unit))]
+        return [
+            part * phase[l, which, q, 0] + pltpu.roll(part, 64, 1) * phase[l, which, q, 1]
+            for part, q in zip(parts, unit)
+        ]
+
+    def pass_on(l, n):
+        at = pl.ds(UNITS[n][0], len(UNITS[n]))
         copy = pltpu.make_async_remote_copy(
-            src_ref=image.at[l, i],
-            dst_ref=image_in.at[l, i],
-            send_sem=send_m.at[l, i],
-            recv_sem=recv_m.at[l, i],
+            src_ref=image.at[l, at],
+            dst_ref=image_in.at[l, at],
+            send_sem=send_m.at[l, n],
+            recv_sem=recv_m.at[l, n],
             device_id={"sub": partners[l]},
             device_id_type=MESH,
         )
         copy.start()
-        m_copies[l, i] = copy
-
-    def step(kind, i):
+        m_copies[l, n] = copy
+
+    def step(kind, n):
+        if kind == "dft":
+            transform(n, n == 0)
+            return
         if kind == "tab":
-            tables(i)
-        elif kind == "perm":
+            tables(n)
+            return
+        if kind == "perm":
             orders()
-        elif kind == "beam":
-            if i == ORDER[0]:
+            return
+        unit = UNITS[n]
+        if kind == "beam":
+            if n == 0:
                 beam_copy.wait()
             for j in (1, 2, 3):
-                a_copies[i, j].wait_recv()
-            own_copies[i].wait()
-            total = jnp.dot(beam[...], got[i].reshape(512, 2 * LANES), preferred_element_type=f32)
-            low, high = [
-                total[:ANG, at] + turned * pltpu.roll(total[ANG:, at], 64, 1)
-                for at in (slice(0, LANES), slice(LANES, 2 * LANES))
-            ]
+                a_copies[n, j].wait_recv()
+            own_copies[n].wait()
+            both = jnp.concatenate([got[q].reshape(512, 2 * LANES) for q in unit], axis=1)
+            total = jnp.dot(beam[...], both, preferred_element_type=f32)
             is_low = x_lo == 0
-            part_out[i] = jnp.where(is_low, high, low).astype(bf16)
+            owned = []
+            for t, q in enumerate(unit):
+                low, high = [
+                    total[:ANG, at] + turned * pltpu.roll(total[ANG:, at], 64, 1)
+                    for at in (slice(2 * t * LANES, (2 * t + 1) * LANES), slice((2 * t + 1) * LANES, (2 * t + 2) * LANES))
+                ]
+                part_out[q] = jnp.where(is_low, high, low).astype(bf16)
+                owned.append(jnp.where(is_low, low, high))
+            at = pl.ds(unit[0], len(unit))
             copy = pltpu.make_async_remote_copy(
-                src_ref=part_out.at[i],
-                dst_ref=part_in.at[i],
-                send_sem=send_x.at[i],
-                recv_sem=recv_x.at[i],
+                src_ref=part_out.at[at],
+                dst_ref=part_in.at[at],
+                send_sem=send_x.at[n],
+                recv_sem=recv_x.at[n],
                 device_id={"rng": x_partner},
                 device_id_type=MESH,
             )
             copy.start()
-            x_copies[i] = copy
-            part_own[i] = jnp.where(is_low, low, high)
+            x_copies[n] = copy
+            for q, value in zip(unit, owned):
+                part_own[q] = value
         elif kind == "lead":
-            x_copies[i].wait_recv()
-            image[0, i] = (part_own[i] + part_in[i].astype(f32)).astype(bf16)
-            pass_on(0, i)
+            x_copies[n].wait_recv()
+            for q in unit:
+                image[0, q] = (part_own[q] + part_in[q].astype(f32)).astype(bf16)
+            pass_on(0, n)
         else:
             l = int(kind[1])
-            m_copies[l, i].wait_recv()
-            merged = (contribution(l, 0, i, image.at[l, i]) + contribution(l, 1, i, image_in.at[l, i])).astype(bf16)
+            m_copies[l, n].wait_recv()
+            mine = contribution(l, 0, unit, image)
+            theirs = contribution(l, 1, unit, image_in)
+            for q, a, b in zip(unit, mine, theirs):
+                merged = a + b
+                if l < MERGES - 1:
+                    image[l + 1, q] = merged.astype(bf16)
+                    continue
+                tile = (q // 2) * LANES
+                if q % 2 == 0:
+                    final[0, :, tile : tile + 64] = merged[:, :64].astype(bf16)
+                    final[1, :, tile + 64 : tile + LANES] = merged[:, 64:].astype(bf16)
+                else:
+                    turn = pltpu.roll(merged, 64, 1)
+                    final[1, :, tile : tile + 64] = turn[:, :64].astype(bf16)
+                    final[0, :, tile + 64 : tile + LANES] = turn[:, 64:].astype(bf16)
             if l < MERGES - 1:
-                image[l + 1, i] = merged
-                pass_on(l + 1, i)
-            else:
-                final[:, i * LANES : (i + 1) * LANES] = merged
+                pass_on(l + 1, n)
 
     turned = jnp.where(lax.broadcasted_iota(jnp.int32, (ANG, LANES), 1) < 64, 1.0, -1.0)
     for kind, i in order_of_steps():
         step(kind, i)
 
     def magnitude(at):
-        re = lax.dot_general(perm[0, at], final[...], (((1,), (1,)), ((), ())), preferred_element_type=f32)
-        im = lax.dot_general(perm[1, at], final[...], (((1,), (1,)), ((), ())), preferred_element_type=f32)
+        re = lax.dot_general(perm[0, at], final[0], (((1,), (1,)), ((), ())), preferred_element_type=f32)
+        im = lax.dot_general(perm[1, at], final[1], (((1,), (1,)), ((), ())), preferred_element_type=f32)
         return jnp.sqrt(re * re + im * im)
 
     halo_copies = []
@@ -357,39 +404,61 @@
         copy.start()
         halo_copies.append(copy)
     level[64:576] = magnitude(slice(64, 576))
-    for copy in halo_copies:
-        copy.wait_recv()
-
-    place = lax.broadcasted_iota(jnp.int32, (8, 8, LANES), 1)
-
-    def backward(v):
-        return jnp.concatenate([v[7 - j : 8 - j] for j in range(8)], axis=0)
-
-    def spread(h, carry):
-        at = pl.ds(pl.multiple_of(h * LANES, LANES), LANES)
-        u = level[:, at].reshape(80, 8, LANES)
-        above = halo_in[0, :, at].astype(f32).reshape(8, 8, LANES)
-        below = halo_in[1, :, at].astype(f32).reshape(8, 8, LANES)
-        below = jnp.where(rng == 0, backward(u[8:16]), below)
-        above = jnp.where(rng == 7, backward(u[64:72]), above)
-        u = jnp.concatenate(
-            [jnp.where(place == 0, below, u[:8]), u[8:72], jnp.where(place == 7, above, u[72:])], axis=0
-        )
+
+    def sweeps(u):
         for sweep in range(SWEEPS):
             diff = u[1:] - u[:-1]
             flux = diff / (2.0 + 0.5 * (diff * diff))
             u = u[1:-1] + (flux[1:] - flux[:-1])
-        smooth[h] = u.reshape(512, LANES)
+        return u
+
+    def spread(h, carry):
+        at = pl.ds(pl.multiple_of(h * LANES, LANES), LANES)
+        out_ref[h] = sweeps(level[:, at].reshape(80, 8, LANES)).reshape(512, LANES)
         return carry
 
     lax.fori_loop(0, 2, spread, 0)
-    for h in range(2):
-        for pair in range(4):
-            both = [smooth[h, pl.ds(2 * pair + t, 64, stride=8), :] for t in range(2)]
-            out_ref[h * LANES : (h + 1) * LANES, pair * LANES : (pair + 1) * LANES] = jnp.concatenate(both, axis=0).T
+    for copy in halo_copies:
+        copy.wait_recv()
+
+    place = lax.broadcasted_iota(jnp.int32, (8, 8, LANES), 1)
+
+    def backward(v):
+        return jnp.concatenate([v[7 - j : 8 - j] for j in range(8)], axis=0)
+
+    def mend(h, carry):
+        at = pl.ds(pl.multiple_of(h * LANES, LANES), LANES)
+        first = level[64:192, at].reshape(16, 8, LANES)
+        last = level[448:576, at].reshape(16, 8, LANES)
+        above = halo_in[0, :, at].astype(f32).reshape(8, 8, LANES)
+        below = halo_in[1, :, at].astype(f32).reshape(8, 8, LANES)
+        below = jnp.where(rng == 0, backward(first[:8]), below)
+        above = jnp.where(rng == 7, backward(last[8:]), above)
+        u = jnp.concatenate(
+            [
+                jnp.where(place == 0, below, last[:8]),
+                jnp.where(place == 0, first[:8], last[8:]),
+                jnp.where(place == 0, first[8:], above),
+            ],
+            axis=0,
+        )
+        u = sweeps(u)
+        head = out_ref[h, 0:64].reshape(8, 8, LANES)
+        out_ref[h, 0:64] = jnp.where(place == 0, u, head).reshape(64, LANES)
+        tail = out_ref[h, 448:512].reshape(8, 8, LANES)
+        out_ref[h, 448:512] = jnp.where(place == 7, u, tail).reshape(64, LANES)
+        return carry
+
+    lax.fori_loop(0, 2, mend, 0)
 
     for copy in list(a_copies.values()) + list(x_copies.values()) + list(m_copies.values()) + halo_copies:
         copy.wait_send()
+
+
+def restore(smooth_ref, out_ref):
+    for pair in range(4):
+        both = [smooth_ref[0, pl.ds(2 * pair + t, 64, stride=8), :] for t in range(2)]
+        out_ref[:, pair * LANES : (pair + 1) * LANES] = jnp.concatenate(both, axis=0).T
 
 
 def per_device(raw_echoes, merge_taps, merge_weights, track_offsets):
@@ -398,18 +467,21 @@
     smem = pl.BlockSpec(memory_space=pltpu.SMEM)
     anywhere = pl.BlockSpec(memory_space=pl.ANY)
     dma = pltpu.SemaphoreType.DMA
-    return pl.pallas_call(
+    smooth = pl.pallas_call(
         kernel,
-        out_shape=jax.ShapeDtypeStruct((ANG, 512), f32),
-        in_specs=[anywhere, anywhere, anywhere, vmem, vmem, vmem, smem],
+        out_shape=jax.ShapeDtypeStruct((2, 512, LANES), f32),
+        in_specs=[anywhere, anywhere, anywhere, anywhere, anywhere, anywhere, smem],
         out_specs=vmem,
         scratch_shapes=[
             pltpu.VMEM((2, 128, 4096), bf16),
             pltpu.VMEM((4, 256, 256), bf16),
             pltpu.VMEM((2 * ANG, 512), bf16),
+            pltpu.VMEM((2, 32, LANES), f32),
+            pltpu.VMEM((MERGES, 2, TAPS, 2 * ANG), jnp.int32),
+            pltpu.VMEM((MERGES, 2, TAPS, 2 * ANG), f32),
             pltpu.VMEM((GROUPS, 128, 256), bf16),
             pltpu.VMEM((4, 128, 256), f32),
-            pltpu.VMEM((CHUNKS, 4, 128, 2 * LANES), bf16),
+            pltpu.VMEM((4, CHUNKS, 128, 2 * LANES), bf16),
             pltpu.VMEM((CHUNKS, 4, 128, 2 * LANES), bf16),
             pltpu.VMEM((CHUNKS, ANG, LANES), bf16),
             pltpu.VMEM((CHUNKS, ANG, LANES), bf16),
@@ -418,20 +490,19 @@
             pltpu.VMEM((MERGES, CHUNKS, ANG, LANES), bf16),
             pltpu.VMEM((MERGES, 2, CHUNKS, 2, ANG, LANES), f32),
             pltpu.VMEM((MERGES, 2, ANG, ANG), bf16),
-            pltpu.VMEM((2, 640, CHUNKS * LANES), bf16),
-            pltpu.VMEM((ANG, CHUNKS * LANES), bf16),
+            pltpu.VMEM((2, 640, 512), bf16),
+            pltpu.VMEM((2, ANG, 512), bf16),
             pltpu.VMEM((640, ANG), f32),
-            pltpu.VMEM((2, 512, LANES), f32),
             pltpu.VMEM((2, 64, ANG), bf16),
             pltpu.VMEM((2, 64, ANG), bf16),
-            dma((4,)),
-            dma((CHUNKS,)),
-            dma((CHUNKS, 3)),
-            dma((CHUNKS, 3)),
-            dma((CHUNKS,)),
-            dma((CHUNKS,)),
-            dma((MERGES, CHUNKS)),
-            dma((MERGES, CHUNKS)),
+            dma((7,)),
+            dma((len(UNITS),)),
+            dma((len(UNITS), 3)),
+            dma((len(UNITS), 3)),
+            dma((len(UNITS),)),
+            dma((len(UNITS),)),
+            dma((MERGES, len(UNITS))),
+            dma((MERGES, len(UNITS))),
             dma((2,)),
             dma((2,)),
         ],
@@ -448,6 +519,14 @@
         merge_weights,
         track_offsets,
     )
+    return pl.pallas_call(
+        restore,
+        grid=(2,),
+        out_shape=jax.ShapeDtypeStruct((ANG, 512), f32),
+        in_specs=[pl.BlockSpec((1, 512, LANES), lambda h: (h, 0, 0))],
+        out_specs=pl.BlockSpec((LANES, 512), lambda h: (h, 0)),
+        name="restore",
+    )(smooth)
 
 
 def solution(mesh):

time: 69 us -> 64.1 us (0.929)
  Pallas kernels: 66.3 us -> 63.6 us
  local copies, waits for them, and re-layouts: 1.87 us -> 0 us
    pallas_call x1 -> x2, Pallas kernels: 66.3 us -> 63.6 us  [the longest x1 61.7 us: per_device(): pl.pallas_call(kernel, out_shape=jax.ShapeDtypeStruct((2, 512, LANES), f3...]
    unnamed x1 -> x0, local copies, waits for them, and re-layouts: 1.87 us -> none
where the time goes in v3:
time: 64.1 us; the launch traced here: 63.7 us
  Pallas kernels  63.6 us (99%)
    pallas_call x1, Pallas kernels, per_device(): pl.pallas_call(kernel, out_shape=jax.ShapeDtypeStruct((2, 512, LANES), f3...  61.7 us
    pallas_call x1, Pallas kernels, per_device(): pl.pallas_call(restore, grid=(2,), out_shape=jax.ShapeDtypeStruct((ANG, 5...  1.95 us

profile of v3, /device:TPU:1, one launch (start us, length us, event | category | flops | bytes accessed | tf_op | source)
XLA Modules:
  0.0 63.7 jit_solution(15745996396910284035)
XLA Ops:
  0.0 61.7 %backproject.1.smooth_ref = f32[2,512,128]{2,1,0:T(8,128)} custom-call(bf16[2,128,4096]{2,1,0:T(8,128)(2,1)} %raw_hbm.1, bf16[4,256,256]{2,1,0:T(8,128)(2,1)} %constant.6.clone.second_hbm, bf16[2,512,512]{2,1,0:T(8,128)(2,1)} %constant.7.clone.beam_hbm, f32[2,32,128]{2,1,0:T(8,128)} %constant.8.clone.twiddle_hbm, s32[4,2,8,512]{3,2,1,0:T(8,128)} %taps_hbm.1, ...), custom_call_target="tpu_custom_call" | custom-call | tf_op jit(solution)/shard_map/backproject/pallas_call | solution.py:470
  61.7 1.9 %restore.1 = f32[256,512]{1,0:T(8,128)} custom-call(f32[2,512,128]{2,1,0:T(8,128)} %backproject.1.smooth_ref), custom_call_target="tpu_custom_call" | custom-call | tf_op jit(solution)/shard_map/restore/pallas_call | solution.py:522

commit v4 on v3

--- a/solution.py
+++ b/solution.py
@@ -184,12 +184,12 @@
         if first:
             twiddle_copy.wait()
             raw_copies[0].wait()
-            lax.fori_loop(0, 4, rows, 0)
+            lax.fori_loop(0, 4, rows, 0, unroll=2)
             raw_copies[1].wait()
-            lax.fori_loop(4, 8, rows, 0)
+            lax.fori_loop(4, 8, rows, 0, unroll=2)
             second_copy.wait()
         else:
-            lax.fori_loop(0, 8, rows, 0)
+            lax.fori_loop(0, 8, rows, 0, unroll=2)
         for odd in range(2):
             for g in range(4):
                 wide[g] = jnp.dot(rows_buf[2 * g + odd], second[g], preferred_element_type=f32)
@@ -206,7 +206,7 @@
                     sent[2 * part + r // 2, i, at, (r % 2) * LANES : (r % 2 + 1) * LANES] = tiles[r].astype(bf16)
             return carry
 
-        lax.fori_loop(0, 8, pick, 0)
+        lax.fori_loop(0, 8, pick, 0, unroll=4)
         if first:
             pl.semaphore_wait(barrier, len(ids))
         for n, unit in enumerate(UNITS):
@@ -270,7 +270,7 @@
                         er, ei = er * tr - ei * ti, er * ti + ei * tr
                 return carry
 
-            lax.fori_loop(0, ANG // 32, fill, 0)
+            lax.fori_loop(0, ANG // 32, fill, 0, unroll=2)
 
     def orders():
         for i in range(4):
@@ -417,7 +417,7 @@
         out_ref[h] = sweeps(level[:, at].reshape(80, 8, LANES)).reshape(512, LANES)
         return carry
 
-    lax.fori_loop(0, 2, spread, 0)
+    lax.fori_loop(0, 2, spread, 0, unroll=True)
     for copy in halo_copies:
         copy.wait_recv()
 
@@ -449,7 +449,7 @@
         out_ref[h, 448:512] = jnp.where(place == 7, u, tail).reshape(64, LANES)
         return carry
 
-    lax.fori_loop(0, 2, mend, 0)
+    lax.fori_loop(0, 2, mend, 0, unroll=True)
 
     for copy in list(a_copies.values()) + list(x_copies.values()) + list(m_copies.values()) + halo_copies:
         copy.wait_send()

time: 64.1 us -> 63.5 us (level)
  no operation moved by 1% of the time
where the time goes in v4:
time: 63.5 us; the launch traced here: 63.4 us
  Pallas kernels  63.4 us (100%)
    pallas_call x1, Pallas kernels, per_device(): pl.pallas_call(kernel, out_shape=jax.ShapeDtypeStruct((2, 512, LANES), f3...  61.5 us
    pallas_call x1, Pallas kernels, per_device(): pl.pallas_call(restore, grid=(2,), out_shape=jax.ShapeDtypeStruct((ANG, 5...  1.95 us

profile of v4, /device:TPU:1, one launch (start us, length us, event | category | flops | bytes accessed | tf_op | source)
XLA Modules:
  0.0 63.4 jit_solution(1820325508909421437)
XLA Ops:
  0.0 61.5 %backproject.1.smooth_ref = f32[2,512,128]{2,1,0:T(8,128)} custom-call(bf16[2,128,4096]{2,1,0:T(8,128)(2,1)} %raw_hbm.1, bf16[4,256,256]{2,1,0:T(8,128)(2,1)} %constant.6.clone.second_hbm, bf16[2,512,512]{2,1,0:T(8,128)(2,1)} %constant.7.clone.beam_hbm, f32[2,32,128]{2,1,0:T(8,128)} %constant.8.clone.twiddle_hbm, s32[4,2,8,512]{3,2,1,0:T(8,128)} %taps_hbm.1, ...), custom_call_target="tpu_custom_call" | custom-call | tf_op jit(solution)/shard_map/backproject/pallas_call | solution.py:470
  61.5 1.9 %restore.1 = f32[256,512]{1,0:T(8,128)} custom-call(f32[2,512,128]{2,1,0:T(8,128)} %backproject.1.smooth_ref), custom_call_target="tpu_custom_call" | custom-call | tf_op jit(solution)/shard_map/restore/pallas_call | solution.py:522
